TPU v7x, 32 devices: a whole 2x2x4 slice. The times are simulated.
32 devices in a mesh: pair: 16 (over z, y, x), rep: 2 (over core).
Axes of the slice: x: 2, y: 2, z: 4, core: 2. Of those that a mesh axis runs over, the one named last changes fastest.
Arguments:
- triplet_pairs: int32 [256, 3], P(('pair', 'rep')), may hold values from 0 to 1023, as said below
- tno_width: int32 [256], P(('pair', 'rep')), may hold values from 64 to 128
- pair_width: int32 [1024], P('pair'), may hold values from 32 to 64
- pair_coeff: bfloat16 [1024, 64, 1024], P('pair'), may hold values from -0.1875 to 0.1875
- pair_amps: bfloat16 [1024, 64, 64], P('pair'), may hold values from -0.03125 to 0.03125
- pair_exch: bfloat16 [1024, 64, 64], P('pair'), may hold values from -0.3125 to 0.3125
- tno_coeff: bfloat16 [256, 1024, 128], P(('pair', 'rep')), may hold values from -0.1875 to 0.1875
- int_left: bfloat16 [256, 3, 128, 128], P(('pair', 'rep')), may hold values from -6 to 6
- int_right: bfloat16 [256, 3, 128, 128], P(('pair', 'rep')), may hold values from -6 to 6
- singles: float32 [256, 3, 128], P(('pair', 'rep')), may hold values from -6 to 6
- tno_energy: float32 [256, 128], P(('pair', 'rep')), may hold values from 0.5 to 5
- gap: float32 [256], P(('pair', 'rep')), may hold values from 1 to 4
Outputs:
- triplet_energy: float32 [256], P(('pair', 'rep'))
- pair_energy: float32 [1024], P('pair')
Inputs may be any that keep to these rules, and one draw needn't show every extreme that they name: `triplet_pairs`: pair p is owned by index p // 64 of axis pair. The triplets of one chip are rows 2 * c * 8 to 2 * (c + 1) * 8 - 1; among their 48 pair ids at most 3 have one owner, and in every chip some owner has exactly 3 of them.
All inputs are finite; a program needn't handle non-finite values.
Results may differ from a plain program's by a relative error of at most 0.00044.
Values may be sent and summed in bfloat16 or wider, within the bound.
A program may use at most 128 MiB of HBM per device.

v0:
```python
import jax
import jax.numpy as jnp
from jax import lax
from jax.sharding import PartitionSpec as P


def projected_energy(
    pno_coeff, pno_blocks, tno_block, tno_count, left, right, single_amps, tno_levels, shift
):
    tno_size = tno_block.shape[1]
    pno_size = pno_coeff.shape[1]
    kept_cols = (jnp.arange(tno_size, dtype=jnp.int32) < tno_count).astype(jnp.float32)
    tno_kept = tno_block * kept_cols.astype(jnp.bfloat16)[None, :]
    intersection = jnp.einsum(
        "xad,db->xab", pno_coeff, tno_kept, preferred_element_type=jnp.float32
    ).astype(jnp.bfloat16)
    halfway = jnp.einsum(
        "xab,xac->xbc", intersection, pno_blocks, preferred_element_type=jnp.float32
    ).astype(jnp.bfloat16)
    halfway = halfway.reshape(3, tno_size, 2, pno_size)
    projected = jnp.einsum(
        "xbkc,xcd->xkbd", halfway, intersection, preferred_element_type=jnp.float32
    )
    amps_tno = projected[:, 0].astype(jnp.bfloat16)
    exch_tno = projected[:, 1]
    left_cols = jnp.transpose(left, (2, 0, 1)).reshape(tno_size, 3 * tno_size)
    right_cols = jnp.transpose(right, (2, 0, 1)).reshape(tno_size, 3 * tno_size)
    khatri = (left_cols[:, None, :] * right_cols[None, :, :]).reshape(
        tno_size * tno_size, 3 * tno_size
    )
    leading = jnp.transpose(amps_tno, (1, 0, 2)).reshape(tno_size, 3 * tno_size)
    connected = lax.dot_general(
        leading, khatri, (((1,), (1,)), ((), ())), preferred_element_type=jnp.float32
    )
    connected = connected.reshape(tno_size, tno_size, tno_size)
    complete = connected + single_amps[0][None, None, :] * exch_tno[0][:, :, None]
    complete = complete + single_amps[1][None, :, None] * exch_tno[1][:, None, :]
    complete = complete + single_amps[2][:, None, None] * exch_tno[2][None, :, :]
    denominator = (
        tno_levels[:, None, None] + tno_levels[None, :, None] + tno_levels[None, None, :] + shift
    )
    cube_mask = kept_cols[:, None, None] * kept_cols[None, :, None] * kept_cols[None, None, :]
    return jnp.sum(cube_mask * connected * complete / denominator)


def owner_ranks(owners):
    matching = owners[:, None] == owners[None, :]
    position = jnp.arange(owners.shape[0], dtype=jnp.int32)
    earlier = position[None, :] < position[:, None]
    return jnp.sum(jnp.logical_and(matching, earlier), axis=1)


def body(
    triplet_pairs,
    tno_width,
    pair_width,
    pair_coeff,
    pair_amps,
    pair_exch,
    tno_coeff,
    int_left,
    int_right,
    singles,
    tno_energy,
    gap,
):
    owner_count = lax.axis_size("pair")
    pair_dev = pair_coeff.shape[0]
    pno_size = pair_coeff.shape[1]
    domain = pair_coeff.shape[2]
    references = triplet_pairs.reshape(-1)
    ref_count = references.shape[0]
    capacity = (2 * ref_count + owner_count - 1) // owner_count
    kept_rows = (jnp.arange(pno_size, dtype=jnp.int32)[None, :] < pair_width[:, None]).astype(
        jnp.bfloat16
    )
    masked = pair_coeff * kept_rows[:, :, None]
    paired = jnp.concatenate([pair_amps, pair_exch], axis=2)
    chip_refs = lax.all_gather(references, "rep", axis=0, tiled=True)
    owners = chip_refs // pair_dev
    slot_rank = owner_ranks(owners)
    requests = (
        jnp.zeros((owner_count * capacity,), jnp.int32)
        .at[owners * capacity + slot_rank]
        .set(chip_refs % pair_dev)
    )
    requests = requests.reshape(owner_count, capacity)
    asked_rows = lax.all_to_all(requests, "pair", split_axis=0, concat_axis=0, tiled=True)
    replica = lax.axis_index("rep")
    coeff_part = lax.dynamic_slice_in_dim(masked, replica * (domain // 2), domain // 2, 2)
    paired_part = lax.dynamic_slice_in_dim(paired, replica * pno_size, pno_size, 2)
    got_coeff, got_paired = (
        lax.all_to_all(coeff_part[asked_rows], "pair", split_axis=0, concat_axis=0, tiled=True),
        lax.all_to_all(paired_part[asked_rows], "pair", split_axis=0, concat_axis=0, tiled=True),
    )
    got_coeff, got_paired = (
        lax.all_gather(got_coeff, "rep", axis=3, tiled=True),
        lax.all_gather(got_paired, "rep", axis=3, tiled=True),
    )
    positions = owners * capacity + slot_rank
    positions = lax.dynamic_slice_in_dim(positions, replica * ref_count, ref_count)
    flat_coeff = got_coeff.reshape(-1, pno_size, domain)
    flat_paired = got_paired.reshape(-1, pno_size, 2 * pno_size)
    trips = tno_coeff.shape[0]
    coeff_trip = flat_coeff[positions].reshape(trips, 3, pno_size, domain)
    paired_trip = flat_paired[positions].reshape(trips, 3, pno_size, 2 * pno_size)

    def single_triplet(items):
        return projected_energy(*items)

    energies = lax.map(
        single_triplet,
        (
            coeff_trip,
            paired_trip,
            tno_coeff,
            tno_width,
            int_left,
            int_right,
            singles,
            tno_energy,
            gap,
        ),
    )
    shares = jnp.repeat(energies / 3.0, 3)
    all_pairs = jnp.arange(owner_count * pair_dev, dtype=jnp.int32)
    dense = jnp.sum(
        jnp.where(references[:, None] == all_pairs[None, :], shares[:, None], 0.0), axis=0
    )
    owned = lax.psum_scatter(dense, "pair", scatter_dimension=0, tiled=True)
    pair_energy = lax.psum(owned, "rep")
    return (energies, pair_energy)


def solution(mesh):
    placed = (
        P(("pair", "rep"), None),
        P(("pair", "rep")),
        P("pair"),
        P("pair", None, None),
        P("pair", None, None),
        P("pair", None, None),
        P(("pair", "rep"), None, None),
        P(("pair", "rep"), None, None, None),
        P(("pair", "rep"), None, None, None),
        P(("pair", "rep"), None, None),
        P(("pair", "rep"), None),
        P(("pair", "rep")),
    )
    return jax.shard_map(
        body, mesh=mesh, in_specs=placed, out_specs=(P(("pair", "rep")), P("pair")), check_vma=False
    )
```

profile of v0, /device:TPU:0, one launch (start us, length us, event | category | flops | bytes accessed | tf_op | source)
XLA Modules:
  0.0 362.0 jit_solution(6125471141535542919)
XLA Ops:
  8.0 1.2 dynamic-slice
  10.2 2.0 all-reduce
  13.7 8.2 %all-to-all-start = ((s32[16,1,3]{2,1,0:T(1,128)}), s32[16,1,3]{2,1,0:T(1,128)S(1)}, u32[]{:S(2)}, u32[]{:S(2)}) async-start(s32[16,1,3]{2,1,0:T(1,128)} %bitcast.29), calls=%async_computation | async-start | bytes 16384 | tf_op jit(solution)/shard_map/all_to_all | solution.py:88
  22.7 4.0 %dynamic-slice_multiply_fusion = bf16[64,64,512]{2,1,0:T(8,128)(2,1)} fusion(bf16[64,64,1024]{2,1,0:T(8,128)(2,1)} %param.17, s32[]{:T(128)S(6)} %select_n.43, bf16[64,64]{1,0:T(8,128)(2,1)S(1)} %fusion.23), kind=kLoop, calls=%fused_computation.43 | loop fusion | flops 8388608 | bytes 8396804 | tf_op jit(solution)/shard_map/mul | solution.py:77
  26.7 2.5 all-to-all-done
  29.5 2.9 gather_fusion
  32.5 75.4 %all_to_all.22 = bf16[16,3,64,512]{3,2,1,0:T(8,128)(2,1)} all-to-all(bf16[16,3,64,512]{3,2,1,0:T(8,128)(2,1)S(1)} %bitcast.110), channel_id=1, replica_groups=mesh['pair'=16,'rep'=2] {'pair'}, dimensions={0} | all-to-all | bytes 6291456 | tf_op jit(solution)/shard_map/all_to_all | solution.py:93
  107.9 2.6 dynamic-slice_maximum_fusion
  111.2 1.3 reshape.272
  112.5 3.9 %all-to-all-start.2 = ((bf16[16,2,6144]{2,1,0:T(2,128)(2,1)}), bf16[16,2,6144]{2,1,0:T(2,128)(2,1)S(1)}, u32[]{:S(2)}, u32[]{:S(2)}) async-start(bf16[16,2,6144]{2,1,0:T(2,128)(2,1)} %reshape.272), calls=%async_computation.2 | async-start | bytes 786432 | tf_op jit(solution)/shard_map/all_to_all | solution.py:94
  117.8 10.5 %all-to-all-done.2 = bf16[16,2,6144]{2,1,0:T(2,128)(2,1)S(1)} async-done(((bf16[16,2,6144]{2,1,0:T(2,128)(2,1)}), bf16[16,2,6144]{2,1,0:T(2,128)(2,1)S(1)}, u32[]{:S(2)}, u32[]{:S(2)}) %all-to-all-start.2) | async-done | bytes 393248 | tf_op jit(solution)/shard_map/all_to_all | solution.py:94
  129.5 2.9 all_gather.11
  132.4 1.2 copy.64
  133.6 1.4 gather_fusion.3
  134.9 3.5 gather_fusion.1
  138.5 174.5 %while.10 = (s32[]{:T(128)}, f32[8]{0:T(128)S(1)}, s32[8]{0:T(128)S(1)}, bf16[8,3,64,1024]{3,2,1,0:T(8,128)(2,1)S(1)}, bf16[8,1024,128]{2,1,0:T(8,128)(2,1)}, /*...) while((s32[]{:T(128)}, f32[8]{0:T(128)S(1)}, ...), condition=%wide.region_4.5_spmd, body=%wide.region_2.4_spmd.sunk | while | flops 1732485504 | bytes 29010464 | solution.py:111
  139.9 1.2 convolution_convert_fusion.4
  141.1 1.0 convolution_convert_fusion.5
  143.9 1.0 constant_dynamic-slice_fusion.7
  147.9 11.6 %fusion.51 = f32[]{:T(128)} fusion(f32[]{:T(128)} %bitcast.103, f32[128]{0:T(128)S(1)} %fusion.49, f32[128,128]{0,1:T(8,128)S(1)} %broadcast_add_fusion.2, f32[128,128]{1,0:T(8,128)S(1)} %copy.77, f32[128]{0:T(128)S(1)} %get-tuple-element.230, f32[128,128]{1,0:T(8,128)} %copy.78, f32[128]{0:T(128)S(1)} %get-tuple-element.232, ...), kind=kOutput, calls=%fused_computation.8.clone.1 | convolution fusion | flops 1663041536 | bytes 625160 | tf_op jit(solution)/shard_map/while/body/eval_jaxpr/dot_general | solution.py:32
  161.7 1.2 convolution_convert_fusion.4
  162.9 1.0 convolution_convert_fusion.5
  165.7 1.0 constant_dynamic-slice_fusion.7
  169.8 11.6 %fusion.51 = f32[]{:T(128)} fusion(f32[]{:T(128)} %bitcast.103, f32[128]{0:T(128)S(1)} %fusion.49, f32[128,128]{0,1:T(8,128)S(1)} %broadcast_add_fusion.2, f32[128,128]{1,0:T(8,128)S(1)} %copy.77, f32[128]{0:T(128)S(1)} %get-tuple-element.230, f32[128,128]{1,0:T(8,128)} %copy.78, f32[128]{0:T(128)S(1)} %get-tuple-element.232, ...), kind=kOutput, calls=%fused_computation.8.clone.1 | convolution fusion | flops 1663041536 | bytes 625160 | tf_op jit(solution)/shard_map/while/body/eval_jaxpr/dot_general | solution.py:32
  183.5 1.2 convolution_convert_fusion.4
  184.7 1.0 convolution_convert_fusion.5
  187.5 1.0 constant_dynamic-slice_fusion.7
  191.6 11.6 %fusion.51 = f32[]{:T(128)} fusion(f32[]{:T(128)} %bitcast.103, f32[128]{0:T(128)S(1)} %fusion.49, f32[128,128]{0,1:T(8,128)S(1)} %broadcast_add_fusion.2, f32[128,128]{1,0:T(8,128)S(1)} %copy.77, f32[128]{0:T(128)S(1)} %get-tuple-element.230, f32[128,128]{1,0:T(8,128)} %copy.78, f32[128]{0:T(128)S(1)} %get-tuple-element.232, ...), kind=kOutput, calls=%fused_computation.8.clone.1 | convolution fusion | flops 1663041536 | bytes 625160 | tf_op jit(solution)/shard_map/while/body/eval_jaxpr/dot_general | solution.py:32
  205.3 1.2 convolution_convert_fusion.4
  206.5 1.0 convolution_convert_fusion.5
  209.3 1.0 constant_dynamic-slice_fusion.7
  213.4 11.6 %fusion.51 = f32[]{:T(128)} fusion(f32[]{:T(128)} %bitcast.103, f32[128]{0:T(128)S(1)} %fusion.49, f32[128,128]{0,1:T(8,128)S(1)} %broadcast_add_fusion.2, f32[128,128]{1,0:T(8,128)S(1)} %copy.77, f32[128]{0:T(128)S(1)} %get-tuple-element.230, f32[128,128]{1,0:T(8,128)} %copy.78, f32[128]{0:T(128)S(1)} %get-tuple-element.232, ...), kind=kOutput, calls=%fused_computation.8.clone.1 | convolution fusion | flops 1663041536 | bytes 625160 | tf_op jit(solution)/shard_map/while/body/eval_jaxpr/dot_general | solution.py:32
  227.1 1.2 convolution_convert_fusion.4
  228.3 1.0 convolution_convert_fusion.5
  235.2 11.6 %fusion.51 = f32[]{:T(128)} fusion(f32[]{:T(128)} %bitcast.103, f32[128]{0:T(128)S(1)} %fusion.49, f32[128,128]{0,1:T(8,128)S(1)} %broadcast_add_fusion.2, f32[128,128]{1,0:T(8,128)S(1)} %copy.77, f32[128]{0:T(128)S(1)} %get-tuple-element.230, f32[128,128]{1,0:T(8,128)} %copy.78, f32[128]{0:T(128)S(1)} %get-tuple-element.232, ...), kind=kOutput, calls=%fused_computation.8.clone.1 | convolution fusion | flops 1663041536 | bytes 625160 | tf_op jit(solution)/shard_map/while/body/eval_jaxpr/dot_general | solution.py:32
  248.9 1.2 convolution_convert_fusion.4
  250.2 1.0 convolution_convert_fusion.5
  253.0 1.0 constant_dynamic-slice_fusion.7
  257.0 11.6 %fusion.51 = f32[]{:T(128)} fusion(f32[]{:T(128)} %bitcast.103, f32[128]{0:T(128)S(1)} %fusion.49, f32[128,128]{0,1:T(8,128)S(1)} %broadcast_add_fusion.2, f32[128,128]{1,0:T(8,128)S(1)} %copy.77, f32[128]{0:T(128)S(1)} %get-tuple-element.230, f32[128,128]{1,0:T(8,128)} %copy.78, f32[128]{0:T(128)S(1)} %get-tuple-element.232, ...), kind=kOutput, calls=%fused_computation.8.clone.1 | convolution fusion | flops 1663041536 | bytes 625160 | tf_op jit(solution)/shard_map/while/body/eval_jaxpr/dot_general | solution.py:32
  270.7 1.2 convolution_convert_fusion.4
  272.0 1.0 convolution_convert_fusion.5
  274.8 1.0 constant_dynamic-slice_fusion.7
  278.8 11.6 %fusion.51 = f32[]{:T(128)} fusion(f32[]{:T(128)} %bitcast.103, f32[128]{0:T(128)S(1)} %fusion.49, f32[128,128]{0,1:T(8,128)S(1)} %broadcast_add_fusion.2, f32[128,128]{1,0:T(8,128)S(1)} %copy.77, f32[128]{0:T(128)S(1)} %get-tuple-element.230, f32[128,128]{1,0:T(8,128)} %copy.78, f32[128]{0:T(128)S(1)} %get-tuple-element.232, ...), kind=kOutput, calls=%fused_computation.8.clone.1 | convolution fusion | flops 1663041536 | bytes 625160 | tf_op jit(solution)/shard_map/while/body/eval_jaxpr/dot_general | solution.py:32
  292.6 1.2 convolution_convert_fusion.4
  293.8 1.0 convolution_convert_fusion.5
  300.6 11.6 %fusion.51 = f32[]{:T(128)} fusion(f32[]{:T(128)} %bitcast.103, f32[128]{0:T(128)S(1)} %fusion.49, f32[128,128]{0,1:T(8,128)S(1)} %broadcast_add_fusion.2, f32[128,128]{1,0:T(8,128)S(1)} %copy.77, f32[128]{0:T(128)S(1)} %get-tuple-element.230, f32[128,128]{1,0:T(8,128)} %copy.78, f32[128]{0:T(128)S(1)} %get-tuple-element.232, ...), kind=kOutput, calls=%fused_computation.8.clone.1 | convolution fusion | flops 1663041536 | bytes 625160 | tf_op jit(solution)/shard_map/while/body/eval_jaxpr/dot_general | solution.py:32
  313.3 38.8 %all-reduce.1 = f32[1024]{0:T(1024)S(1)} all-reduce(f32[1024]{0:T(1024)S(1)} %select_reduce_fusion), channel_id=2, replica_groups=mesh['pair'=16,'rep'=2] {'pair'}, use_global_device_ids=true, to_apply=%region_6.7.clone | all-reduce | flops 1024 | bytes 8192
  352.2 2.9 psum.7
  (192 shorter events, 63.6 us)
Async XLA Ops:
  13.7 15.5 %all-to-all-start = ((s32[16,1,3]{2,1,0:T(1,128)}), s32[16,1,3]{2,1,0:T(1,128)S(1)}, u32[]{:S(2)}, u32[]{:S(2)}) async-start(s32[16,1,3]{2,1,0:T(1,128)} %bitcast.29), calls=%async_computation | async-start | bytes 16384 | tf_op jit(solution)/shard_map/all_to_all | solution.py:88
  21.9 113.0 %all-gather.2.cloned.1.call-start = ((), (), s32[]{:S(2)}) async-start(), calls=%async_computation.3 | async-start | bytes 9437184 | tf_op jit(solution)/shard_map/all_gather | solution.py:97
  32.5 84.0 %copy-start.4 = (u32[32]{0:T(128)S(1)}, u32[32]{0:T(128)}, u32[]{:S(2)}) copy-start(u32[32]{0:T(128)} %constant.93) | copy-start | bytes 388
  111.2 27.3 %copy-start.2 = (s32[8]{0:T(128)S(1)}, s32[8]{0:T(128)}, u32[]{:S(2)}) copy-start(s32[8]{0:T(128)} %param.15) | copy-start | bytes 100
  111.2 27.3 %copy-start.3 = (f32[8]{0:T(128)S(1)}, f32[8]{0:T(128)}, u32[]{:S(2)}) copy-start(f32[8]{0:T(128)} %param.25) | copy-start | bytes 100
  112.5 15.8 %all-to-all-start.2 = ((bf16[16,2,6144]{2,1,0:T(2,128)(2,1)}), bf16[16,2,6144]{2,1,0:T(2,128)(2,1)S(1)}, u32[]{:S(2)}, u32[]{:S(2)}) async-start(bf16[16,2,6144]{2,1,0:T(2,128)(2,1)} %reshape.272), calls=%async_computation.2 | async-start | bytes 786432 | tf_op jit(solution)/shard_map/all_to_all | solution.py:94
  138.5 3.6 %copy-start = (bf16[8,3,64,1024]{3,2,1,0:T(8,128)(2,1)}, bf16[8,3,64,1024]{3,2,1,0:T(8,128)(2,1)S(1)}, u32[]{:S(2)}) copy-start(bf16[8,3,64,1024]{3,2,1,0:T(8,128)(2,1)S(1)} %get-tuple-element.271) | copy-start | bytes 9437188 | tf_op jit(solution)/shard_map/while
  147.9 12.4 %copy-start.1 = (bf16[8,3,64,1024]{3,2,1,0:T(8,128)(2,1)S(1)}, bf16[8,3,64,1024]{3,2,1,0:T(8,128)(2,1)}, u32[]{:S(2)}) copy-start(bf16[8,3,64,1024]{3,2,1,0:T(8,128)(2,1)} %copy-done) | copy-start | bytes 9437188 | tf_op jit(solution)/shard_map/while
  160.3 3.6 copy-start
  169.8 12.4 %copy-start.1 = (bf16[8,3,64,1024]{3,2,1,0:T(8,128)(2,1)S(1)}, bf16[8,3,64,1024]{3,2,1,0:T(8,128)(2,1)}, u32[]{:S(2)}) copy-start(bf16[8,3,64,1024]{3,2,1,0:T(8,128)(2,1)} %copy-done) | copy-start | bytes 9437188 | tf_op jit(solution)/shard_map/while
  182.2 3.6 copy-start
  191.6 12.4 %copy-start.1 = (bf16[8,3,64,1024]{3,2,1,0:T(8,128)(2,1)S(1)}, bf16[8,3,64,1024]{3,2,1,0:T(8,128)(2,1)}, u32[]{:S(2)}) copy-start(bf16[8,3,64,1024]{3,2,1,0:T(8,128)(2,1)} %copy-done) | copy-start | bytes 9437188 | tf_op jit(solution)/shard_map/while
  204.0 3.6 copy-start
  213.4 12.4 %copy-start.1 = (bf16[8,3,64,1024]{3,2,1,0:T(8,128)(2,1)S(1)}, bf16[8,3,64,1024]{3,2,1,0:T(8,128)(2,1)}, u32[]{:S(2)}) copy-start(bf16[8,3,64,1024]{3,2,1,0:T(8,128)(2,1)} %copy-done) | copy-start | bytes 9437188 | tf_op jit(solution)/shard_map/while
  225.8 3.6 copy-start
  235.2 12.4 %copy-start.1 = (bf16[8,3,64,1024]{3,2,1,0:T(8,128)(2,1)S(1)}, bf16[8,3,64,1024]{3,2,1,0:T(8,128)(2,1)}, u32[]{:S(2)}) copy-start(bf16[8,3,64,1024]{3,2,1,0:T(8,128)(2,1)} %copy-done) | copy-start | bytes 9437188 | tf_op jit(solution)/shard_map/while
  247.6 3.6 copy-start
  257.0 12.4 %copy-start.1 = (bf16[8,3,64,1024]{3,2,1,0:T(8,128)(2,1)S(1)}, bf16[8,3,64,1024]{3,2,1,0:T(8,128)(2,1)}, u32[]{:S(2)}) copy-start(bf16[8,3,64,1024]{3,2,1,0:T(8,128)(2,1)} %copy-done) | copy-start | bytes 9437188 | tf_op jit(solution)/shard_map/while
  269.4 3.6 copy-start
  278.8 12.4 %copy-start.1 = (bf16[8,3,64,1024]{3,2,1,0:T(8,128)(2,1)S(1)}, bf16[8,3,64,1024]{3,2,1,0:T(8,128)(2,1)}, u32[]{:S(2)}) copy-start(bf16[8,3,64,1024]{3,2,1,0:T(8,128)(2,1)} %copy-done) | copy-start | bytes 9437188 | tf_op jit(solution)/shard_map/while
  291.2 3.6 copy-start
  300.6 12.4 %copy-start.1 = (bf16[8,3,64,1024]{3,2,1,0:T(8,128)(2,1)S(1)}, bf16[8,3,64,1024]{3,2,1,0:T(8,128)(2,1)}, u32[]{:S(2)}) copy-start(bf16[8,3,64,1024]{3,2,1,0:T(8,128)(2,1)} %copy-done) | copy-start | bytes 9437188 | tf_op jit(solution)/shard_map/while
  313.0 42.1 %copy-start.5 = (f32[8]{0:T(128)}, f32[8]{0:T(128)S(1)}, u32[]{:S(2)}) copy-start(f32[8]{0:T(128)S(1)} %get-tuple-element.57) | copy-start | bytes 100
Sparse Core Ops, SparseCore 0:
  108.0 15.0 all-gather.1
where the time goes:
time: 364 us; the launch traced here: 362 us
  blocking collectives  122 us (34%)
  matrix products  113 us (31%)
  local copies, waits for them, and re-layouts  65.8 us (18%)
  other arithmetic  19.6 us (5%)
  between operations  15.5 us (4%)
  waiting for transfers between devices  13 us (4%)
  starting transfers between devices  12.2 us (3%)
    dot_general x8, matrix products, projected_energy(): lax.dot_general(leading, khatri, (((1,), (1,)), ((), ())), preferred_elem...  93.2 us
    all_to_all x1, blocking collectives, body(): lax.all_to_all(coeff_part[asked_rows], 'pair', split_axis=0, concat_axis=...  75.4 us
    unnamed x2, blocking collectives  40.8 us
    dynamic_slice x24, local copies, waits for them, and re-layouts, body(): lax.map(single_triplet, (coeff_trip, paired_trip, tno_coeff, tno_width, i...  17.7 us
    mul x16, local copies, waits for them, and re-layouts, projected_energy(): single_amps[0][None, None, :] * exch_tno[0][:, :, None]  10.9 us
    all_to_all x1, waiting for transfers between devices, body(): lax.all_to_all(paired_part[asked_rows], 'pair', split_axis=0, concat_axis...  10.5 us
    dot_general x8, matrix products, projected_energy(): jnp.einsum('xad,db->xab', pno_coeff, tno_kept, preferred_element_type=jnp...  9.65 us
    dot_general x8, matrix products, projected_energy(): jnp.einsum('xab,xac->xbc', intersection, pno_blocks, preferred_element_ty...  8.29 us
  transfers between devices with their start and end apart: 3, of which 2 were waited for; matrix products, arithmetic and copies ran while one was open for 4% of the time, Pallas kernels for 0%

commit v1 on v0

--- a/solution.py
+++ b/solution.py
@@ -2,6 +2,27 @@
 import jax.numpy as jnp
 from jax import lax
 from jax.sharding import PartitionSpec as P
+from jax.lax import axis_index, axis_size, ppermute
+
+
+def fill_edge_in(array_here, where_dim, row_data):
+    out_arr = array_here.shape
+    e_now = array_here.reshape(
+        *out_arr[:where_dim], row_data, out_arr[where_dim] // row_data, *out_arr[where_dim + 1 :]
+    )
+    ready = jnp.moveaxis(e_now, where_dim, 0)
+    return ready
+
+
+def search_rings_here(state, axis_no):
+    state = jnp.moveaxis(state, 0, axis_no)
+    everything = state.shape
+    mat_out = state.reshape(
+        *everything[:axis_no],
+        everything[axis_no] * everything[axis_no + 1],
+        *everything[axis_no + 2 :]
+    )
+    return mat_out
 
 
 def projected_energy(
@@ -64,6 +85,24 @@
     tno_energy,
     gap,
 ):
+
+    def view_write(block_here, net_axis, m, x_part):
+        known = axis_size(net_axis)
+        row_out = axis_index(net_axis)
+        q_next, response = (known, row_out)
+        top = fill_edge_in(block_here, m, q_next)
+        nodes = [top[response]]
+        for kk in [*range(1, q_next)]:
+            after = top[response ^ kk]
+            current_value = ppermute(
+                after, net_axis, [(dev_j, dev_j ^ kk) for dev_j in range(q_next)]
+            )
+            nodes.append(current_value)
+        x_new = jnp.stack(nodes, axis=0)
+        top = x_new[response ^ jnp.arange(q_next)]
+        w1 = search_rings_here(top, x_part)
+        return w1
+
     owner_count = lax.axis_size("pair")
     pair_dev = pair_coeff.shape[0]
     pno_size = pair_coeff.shape[1]
@@ -90,7 +129,7 @@
     coeff_part = lax.dynamic_slice_in_dim(masked, replica * (domain // 2), domain // 2, 2)
     paired_part = lax.dynamic_slice_in_dim(paired, replica * pno_size, pno_size, 2)
     got_coeff, got_paired = (
-        lax.all_to_all(coeff_part[asked_rows], "pair", split_axis=0, concat_axis=0, tiled=True),
+        view_write(coeff_part[asked_rows], "pair", 0, 0),
         lax.all_to_all(paired_part[asked_rows], "pair", split_axis=0, concat_axis=0, tiled=True),
     )
     got_coeff, got_paired = (

time: 364 us -> 376 us (1.033)
  blocking collectives: 122 us -> 46.9 us
  starting transfers between devices: 12.2 us -> 48.5 us
  waiting for transfers between devices: 13 us -> 48.2 us
  local copies, waits for them, and re-layouts: 65.8 us -> 82.3 us
    all_to_all x1 -> x0, blocking collectives: 75.4 us -> none  [body(): lax.all_to_all(coeff_part[asked_rows], 'pair', split_axis=0, concat_axis=...]
    ppermute x0 -> x15, waiting for transfers between devices: none -> 37.3 us  [view_write(): ppermute(after, net_axis, [(dev_j, dev_j ^ kk) for dev_j in range(q_next)])]
    ppermute x0 -> x15, starting transfers between devices: none -> 25.3 us  [view_write(): ppermute(after, net_axis, [(dev_j, dev_j ^ kk) for dev_j in range(q_next)])]
    unnamed x15 -> x32, local copies, waits for them, and re-layouts: 4.71 us -> 16.3 us
    all_to_all x1, starting transfers between devices: 3.95 us -> 15 us  [body(): lax.all_to_all(paired_part[asked_rows], 'pair', split_axis=0, concat_axis...]
    gather x0 -> x1, local copies, waits for them, and re-layouts: none -> 4.34 us  [view_write(): top = x_new[response ^ jnp.arange(q_next)]]
  transfers between devices with their start and end apart: 3 -> 18, of which waited for: 2 -> 10; matrix products, arithmetic and copies ran while one was open for 4% -> 6% of each run, Pallas kernels for 0% -> 0%
where the time goes in v1:
time: 376 us; the launch traced here: 374 us
  matrix products  113 us (30%)
  local copies, waits for them, and re-layouts  82.3 us (22%)
  starting transfers between devices  48.5 us (13%)
  waiting for transfers between devices  48.2 us (13%)
  blocking collectives  46.9 us (12%)
  other arithmetic  19.2 us (5%)
  between operations  15.6 us (4%)
    dot_general x8, matrix products, projected_energy(): lax.dot_general(leading, khatri, (((1,), (1,)), ((), ())), preferred_elem...  93 us
    unnamed x2, blocking collectives  41 us
    ppermute x15, waiting for transfers between devices, view_write(): ppermute(after, net_axis, [(dev_j, dev_j ^ kk) for dev_j in range(q_next)])  37.3 us
    ppermute x15, starting transfers between devices, view_write(): ppermute(after, net_axis, [(dev_j, dev_j ^ kk) for dev_j in range(q_next)])  25.3 us
    dynamic_slice x24, local copies, waits for them, and re-layouts, body(): lax.map(single_triplet, (coeff_trip, paired_trip, tno_coeff, tno_width, i...  17.8 us
    unnamed x32, local copies, waits for them, and re-layouts  16.3 us
    all_to_all x1, starting transfers between devices, body(): lax.all_to_all(paired_part[asked_rows], 'pair', split_axis=0, concat_axis...  15 us
    mul x16, local copies, waits for them, and re-layouts, projected_energy(): single_amps[0][None, None, :] * exch_tno[0][:, :, None]  10.9 us
  transfers between devices with their start and end apart: 18, of which 10 were waited for; matrix products, arithmetic and copies ran while one was open for 6% of the time, Pallas kernels for 0%

profile of v1, /device:TPU:0, one launch (start us, length us, event | category | flops | bytes accessed | tf_op | source)
XLA Modules:
  0.0 374.3 jit_solution(1430905789480775947)
XLA Ops:
  8.0 1.2 dynamic-slice.19
  10.2 2.0 all-reduce
  13.7 8.2 %all-to-all-start = ((s32[16,1,3]{2,1,0:T(1,128)}), s32[16,1,3]{2,1,0:T(1,128)S(1)}, u32[]{:S(2)}, u32[]{:S(2)}) async-start(s32[16,1,3]{2,1,0:T(1,128)} %bitcast.29), calls=%async_computation | async-start | bytes 16384 | tf_op jit(solution)/shard_map/all_to_all | solution.py:127
  22.8 4.0 %dynamic-slice_multiply_fusion = bf16[64,64,512]{2,1,0:T(8,128)(2,1)} fusion(bf16[64,64,1024]{2,1,0:T(8,128)(2,1)} %param.17, s32[]{:T(128)S(6)} %select_n.101, bf16[64,64]{1,0:T(8,128)(2,1)S(1)} %fusion.23), kind=kLoop, calls=%fused_computation.44 | loop fusion | flops 8388608 | bytes 8396804 | tf_op jit(solution)/shard_map/mul | solution.py:116
  26.9 2.4 all-to-all-done
  29.5 2.9 gather_fusion
  34.0 2.3 collective-permute-start.2
  37.0 1.5 collective-permute-start.4
  39.1 3.5 collective-permute-done
  43.4 2.5 collective-permute-start.6
  48.3 3.1 collective-permute-start.8
  52.2 2.3 collective-permute-done.4
  55.1 3.8 %collective-permute-done.5 = bf16[1,3,64,512]{3,2,1,0:T(8,128)(2,1)S(1)} collective-permute-done((bf16[1,3,64,512]{3,2,1,0:T(8,128)(2,1)S(1)}, bf16[1,3,64,512]{3,2,1,0:T(8,128)(2,1)S(1)}, u32[]{:S(2)}, u32[]{:S(2)}) %collective-permute-start.5) | collective-permute-done | bytes 196640 | tf_op jit(solution)/shard_map/ppermute | solution.py:97
  58.9 1.5 collective-permute-start.10
  61.1 2.2 collective-permute-done.6
  65.2 15.3 %collective-permute-done.7 = bf16[1,3,64,512]{3,2,1,0:T(8,128)(2,1)S(1)} collective-permute-done((bf16[1,3,64,512]{3,2,1,0:T(8,128)(2,1)S(1)}, bf16[1,3,64,512]{3,2,1,0:T(8,128)(2,1)S(1)}, u32[]{:S(2)}, u32[]{:S(2)}) %collective-permute-start.7) | collective-permute-done | bytes 196640 | tf_op jit(solution)/shard_map/ppermute | solution.py:97
  80.5 3.7 collective-permute-start.12
  86.0 2.5 collective-permute-start.13
  89.2 7.2 %collective-permute-done.9 = bf16[1,3,64,512]{3,2,1,0:T(8,128)(2,1)S(1)} collective-permute-done((bf16[1,3,64,512]{3,2,1,0:T(8,128)(2,1)S(1)}, bf16[1,3,64,512]{3,2,1,0:T(8,128)(2,1)S(1)}, u32[]{:S(2)}, u32[]{:S(2)}) %collective-permute-start.9) | collective-permute-done | bytes 196640 | tf_op jit(solution)/shard_map/ppermute | solution.py:97
  96.4 4.1 %collective-permute-start.14 = (bf16[1,3,64,512]{3,2,1,0:T(8,128)(2,1)S(1)}, bf16[1,3,64,512]{3,2,1,0:T(8,128)(2,1)S(1)}, u32[]{:S(2)}, u32[]{:S(2)}) collective-permute-start(bf16[1,3,64,512]{3,2,1,0:T(8,128)(2,1)S(1)} %get-tuple-element.149), channel_id=1, source_target_pairs={{0,30},{2,28},{4,26},{6,24},{8,22},{10,20},{12,18},{14,16},{16,14}... | collective-permute-start | bytes 589832 | tf_op jit(solution)/shard_map/ppermute | solution.py:97
  104.0 1.8 collective-permute-done.14
  106.5 4.3 %gather_fusion.1 = bf16[16,3,64,512]{3,2,1,0:T(8,128)(2,1)} fusion(bf16[16,3,64,512]{3,2,1,0:T(8,128)(2,1)} %bitcast.48, s32[1024]{0:T(1024)S(1)} %pad_clamp_fusion.1), kind=kCustom, calls=%fused_computation.1 | custom fusion | bytes 6291520 | tf_op jit(solution)/shard_map/gather | solution.py:102
  112.1 2.3 dynamic-slice_maximum_fusion
  115.1 1.3 reshape.335
  116.4 15.0 %all-to-all-start.1 = ((bf16[16,2,6144]{2,1,0:T(2,128)(2,1)}), bf16[16,2,6144]{2,1,0:T(2,128)(2,1)S(1)}, u32[]{:S(2)}, u32[]{:S(2)}) async-start(bf16[16,2,6144]{2,1,0:T(2,128)(2,1)} %reshape.335), calls=%async_computation.1 | async-start | bytes 786432 | tf_op jit(solution)/shard_map/all_to_all | solution.py:133
  132.8 8.5 %all-to-all-done.1 = bf16[16,2,6144]{2,1,0:T(2,128)(2,1)S(1)} async-done(((bf16[16,2,6144]{2,1,0:T(2,128)(2,1)}), bf16[16,2,6144]{2,1,0:T(2,128)(2,1)S(1)}, u32[]{:S(2)}, u32[]{:S(2)}) %all-to-all-start.1) | async-done | bytes 393248 | tf_op jit(solution)/shard_map/all_to_all | solution.py:133
  142.4 2.9 all_gather.11
  146.5 1.4 gather_fusion.4
  147.9 3.6 gather_fusion.2
  151.5 173.6 %while.10 = (s32[]{:T(128)}, f32[8]{0:T(128)S(1)}, s32[8]{0:T(128)S(1)}, bf16[8,3,64,1024]{3,2,1,0:T(8,128)(2,1)S(1)}, bf16[8,1024,128]{2,1,0:T(8,128)(2,1)}, /*...) while((s32[]{:T(128)}, f32[8]{0:T(128)S(1)}, ...), condition=%wide.region_4.5_spmd, body=%wide.region_2.4_spmd.sunk | while | flops 1732485504 | bytes 29010464 | solution.py:150
  152.9 1.2 convolution_convert_fusion.4
  160.9 11.6 %fusion.52 = f32[]{:T(128)} fusion(f32[]{:T(128)} %bitcast.138, f32[128]{0:T(128)S(1)} %fusion.50, f32[128,128]{0,1:T(8,128)S(1)} %broadcast_add_fusion.2, f32[128,128]{1,0:T(8,128)S(1)} %copy.77, f32[128]{0:T(128)S(1)} %get-tuple-element.245, f32[128,128]{1,0:T(8,128)} %copy.78, f32[128]{0:T(128)S(1)} %get-tuple-element.247, ...), kind=kOutput, calls=%fused_computation.9.clone.1 | convolution fusion | flops 1663041536 | bytes 625160 | tf_op jit(solution)/shard_map/while/body/eval_jaxpr/dot_general | solution.py:53
  174.6 1.2 convolution_convert_fusion.4
  182.6 11.6 %fusion.52 = f32[]{:T(128)} fusion(f32[]{:T(128)} %bitcast.138, f32[128]{0:T(128)S(1)} %fusion.50, f32[128,128]{0,1:T(8,128)S(1)} %broadcast_add_fusion.2, f32[128,128]{1,0:T(8,128)S(1)} %copy.77, f32[128]{0:T(128)S(1)} %get-tuple-element.245, f32[128,128]{1,0:T(8,128)} %copy.78, f32[128]{0:T(128)S(1)} %get-tuple-element.247, ...), kind=kOutput, calls=%fused_computation.9.clone.1 | convolution fusion | flops 1663041536 | bytes 625160 | tf_op jit(solution)/shard_map/while/body/eval_jaxpr/dot_general | solution.py:53
  196.3 1.2 convolution_convert_fusion.4
  204.3 11.6 %fusion.52 = f32[]{:T(128)} fusion(f32[]{:T(128)} %bitcast.138, f32[128]{0:T(128)S(1)} %fusion.50, f32[128,128]{0,1:T(8,128)S(1)} %broadcast_add_fusion.2, f32[128,128]{1,0:T(8,128)S(1)} %copy.77, f32[128]{0:T(128)S(1)} %get-tuple-element.245, f32[128,128]{1,0:T(8,128)} %copy.78, f32[128]{0:T(128)S(1)} %get-tuple-element.247, ...), kind=kOutput, calls=%fused_computation.9.clone.1 | convolution fusion | flops 1663041536 | bytes 625160 | tf_op jit(solution)/shard_map/while/body/eval_jaxpr/dot_general | solution.py:53
  218.0 1.2 convolution_convert_fusion.4
  226.0 11.6 %fusion.52 = f32[]{:T(128)} fusion(f32[]{:T(128)} %bitcast.138, f32[128]{0:T(128)S(1)} %fusion.50, f32[128,128]{0,1:T(8,128)S(1)} %broadcast_add_fusion.2, f32[128,128]{1,0:T(8,128)S(1)} %copy.77, f32[128]{0:T(128)S(1)} %get-tuple-element.245, f32[128,128]{1,0:T(8,128)} %copy.78, f32[128]{0:T(128)S(1)} %get-tuple-element.247, ...), kind=kOutput, calls=%fused_computation.9.clone.1 | convolution fusion | flops 1663041536 | bytes 625160 | tf_op jit(solution)/shard_map/while/body/eval_jaxpr/dot_general | solution.py:53
  239.7 1.2 convolution_convert_fusion.4
  247.7 11.6 %fusion.52 = f32[]{:T(128)} fusion(f32[]{:T(128)} %bitcast.138, f32[128]{0:T(128)S(1)} %fusion.50, f32[128,128]{0,1:T(8,128)S(1)} %broadcast_add_fusion.2, f32[128,128]{1,0:T(8,128)S(1)} %copy.77, f32[128]{0:T(128)S(1)} %get-tuple-element.245, f32[128,128]{1,0:T(8,128)} %copy.78, f32[128]{0:T(128)S(1)} %get-tuple-element.247, ...), kind=kOutput, calls=%fused_computation.9.clone.1 | convolution fusion | flops 1663041536 | bytes 625160 | tf_op jit(solution)/shard_map/while/body/eval_jaxpr/dot_general | solution.py:53
  261.4 1.2 convolution_convert_fusion.4
  269.4 11.6 %fusion.52 = f32[]{:T(128)} fusion(f32[]{:T(128)} %bitcast.138, f32[128]{0:T(128)S(1)} %fusion.50, f32[128,128]{0,1:T(8,128)S(1)} %broadcast_add_fusion.2, f32[128,128]{1,0:T(8,128)S(1)} %copy.77, f32[128]{0:T(128)S(1)} %get-tuple-element.245, f32[128,128]{1,0:T(8,128)} %copy.78, f32[128]{0:T(128)S(1)} %get-tuple-element.247, ...), kind=kOutput, calls=%fused_computation.9.clone.1 | convolution fusion | flops 1663041536 | bytes 625160 | tf_op jit(solution)/shard_map/while/body/eval_jaxpr/dot_general | solution.py:53
  283.1 1.2 convolution_convert_fusion.4
  291.1 11.6 %fusion.52 = f32[]{:T(128)} fusion(f32[]{:T(128)} %bitcast.138, f32[128]{0:T(128)S(1)} %fusion.50, f32[128,128]{0,1:T(8,128)S(1)} %broadcast_add_fusion.2, f32[128,128]{1,0:T(8,128)S(1)} %copy.77, f32[128]{0:T(128)S(1)} %get-tuple-element.245, f32[128,128]{1,0:T(8,128)} %copy.78, f32[128]{0:T(128)S(1)} %get-tuple-element.247, ...), kind=kOutput, calls=%fused_computation.9.clone.1 | convolution fusion | flops 1663041536 | bytes 625160 | tf_op jit(solution)/shard_map/while/body/eval_jaxpr/dot_general | solution.py:53
  304.8 1.2 convolution_convert_fusion.4
  312.8 11.6 %fusion.52 = f32[]{:T(128)} fusion(f32[]{:T(128)} %bitcast.138, f32[128]{0:T(128)S(1)} %fusion.50, f32[128,128]{0,1:T(8,128)S(1)} %broadcast_add_fusion.2, f32[128,128]{1,0:T(8,128)S(1)} %copy.77, f32[128]{0:T(128)S(1)} %get-tuple-element.245, f32[128,128]{1,0:T(8,128)} %copy.78, f32[128]{0:T(128)S(1)} %get-tuple-element.247, ...), kind=kOutput, calls=%fused_computation.9.clone.1 | convolution fusion | flops 1663041536 | bytes 625160 | tf_op jit(solution)/shard_map/while/body/eval_jaxpr/dot_general | solution.py:53
  325.4 39.1 %all-reduce.1 = f32[1024]{0:T(1024)S(1)} all-reduce(f32[1024]{0:T(1024)S(1)} %select_reduce_fusion), channel_id=3, replica_groups=mesh['pair'=16,'rep'=2] {'pair'}, use_global_device_ids=true, to_apply=%region_6.7.clone | all-reduce | flops 1024 | bytes 8192
  364.5 2.9 psum.7
  (243 shorter events, 96.0 us)
Async XLA Ops:
  13.7 15.5 %all-to-all-start = ((s32[16,1,3]{2,1,0:T(1,128)}), s32[16,1,3]{2,1,0:T(1,128)S(1)}, u32[]{:S(2)}, u32[]{:S(2)}) async-start(s32[16,1,3]{2,1,0:T(1,128)} %bitcast.29), calls=%async_computation | async-start | bytes 16384 | tf_op jit(solution)/shard_map/all_to_all | solution.py:127
  21.9 125.9 %all-gather.3.cloned.1.call-start = ((), (), s32[]{:S(2)}) async-start(), calls=%async_computation.2 | async-start | bytes 9437184 | tf_op jit(solution)/shard_map/all_gather | solution.py:136
  32.8 9.8 %collective-permute-start = (bf16[1,3,64,512]{3,2,1,0:T(8,128)(2,1)S(1)}, bf16[1,3,64,512]{3,2,1,0:T(8,128)(2,1)S(1)}, u32[]{:S(2)}, u32[]{:S(2)}) collective-permute-start(bf16[1,3,64,512]{3,2,1,0:T(8,128)(2,1)S(1)} %get-tuple-element.163), channel_id=1, source_target_pairs={{0,2},{2,0},{4,6},{6,4},{8,10},{10,8},{12,14},{14,12},{16,18},{18,... | collective-permute-start | bytes 589832 | tf_op jit(solution)/shard_map/ppermute | solution.py:97
  33.5 9.9 %collective-permute-start.1 = (bf16[1,3,64,512]{3,2,1,0:T(8,128)(2,1)S(1)}, bf16[1,3,64,512]{3,2,1,0:T(8,128)(2,1)S(1)}, u32[]{:S(2)}, u32[]{:S(2)}) collective-permute-start(bf16[1,3,64,512]{3,2,1,0:T(8,128)(2,1)S(1)} %get-tuple-element.162), channel_id=1, source_target_pairs={{0,4},{2,6},{4,0},{6,2},{8,12},{10,14},{12,8},{14,10},{16,20},{18,... | collective-permute-start | bytes 589832 | tf_op jit(solution)/shard_map/ppermute | solution.py:97
  34.0 12.5 %collective-permute-start.2 = (bf16[1,3,64,512]{3,2,1,0:T(8,128)(2,1)S(1)}, bf16[1,3,64,512]{3,2,1,0:T(8,128)(2,1)S(1)}, u32[]{:S(2)}, u32[]{:S(2)}) collective-permute-start(bf16[1,3,64,512]{3,2,1,0:T(8,128)(2,1)S(1)} %get-tuple-element.161), channel_id=1, source_target_pairs={{0,6},{2,4},{4,2},{6,0},{8,14},{10,12},{12,10},{14,8},{16,22},{18,... | collective-permute-start | bytes 589832 | tf_op jit(solution)/shard_map/ppermute | solution.py:97
  36.4 11.9 %collective-permute-start.3 = (bf16[1,3,64,512]{3,2,1,0:T(8,128)(2,1)S(1)}, bf16[1,3,64,512]{3,2,1,0:T(8,128)(2,1)S(1)}, u32[]{:S(2)}, u32[]{:S(2)}) collective-permute-start(bf16[1,3,64,512]{3,2,1,0:T(8,128)(2,1)S(1)} %get-tuple-element.160), channel_id=1, source_target_pairs={{0,8},{2,10},{4,12},{6,14},{8,0},{10,2},{12,4},{14,6},{16,24},{18,... | collective-permute-start | bytes 589832 | tf_op jit(solution)/shard_map/ppermute | solution.py:97
  37.0 17.5 %collective-permute-start.4 = (bf16[1,3,64,512]{3,2,1,0:T(8,128)(2,1)S(1)}, bf16[1,3,64,512]{3,2,1,0:T(8,128)(2,1)S(1)}, u32[]{:S(2)}, u32[]{:S(2)}) collective-permute-start(bf16[1,3,64,512]{3,2,1,0:T(8,128)(2,1)S(1)} %get-tuple-element.159), channel_id=1, source_target_pairs={{0,10},{2,8},{4,14},{6,12},{8,2},{10,0},{12,6},{14,4},{16,26},{18,... | collective-permute-start | bytes 589832 | tf_op jit(solution)/shard_map/ppermute | solution.py:97
  42.7 16.3 %collective-permute-start.5 = (bf16[1,3,64,512]{3,2,1,0:T(8,128)(2,1)S(1)}, bf16[1,3,64,512]{3,2,1,0:T(8,128)(2,1)S(1)}, u32[]{:S(2)}, u32[]{:S(2)}) collective-permute-start(bf16[1,3,64,512]{3,2,1,0:T(8,128)(2,1)S(1)} %get-tuple-element.158), channel_id=1, source_target_pairs={{0,12},{2,14},{4,8},{6,10},{8,4},{10,6},{12,0},{14,2},{16,28},{18,... | collective-permute-start | bytes 589832 | tf_op jit(solution)/shard_map/ppermute | solution.py:97
  43.4 20.0 %collective-permute-start.6 = (bf16[1,3,64,512]{3,2,1,0:T(8,128)(2,1)S(1)}, bf16[1,3,64,512]{3,2,1,0:T(8,128)(2,1)S(1)}, u32[]{:S(2)}, u32[]{:S(2)}) collective-permute-start(bf16[1,3,64,512]{3,2,1,0:T(8,128)(2,1)S(1)} %get-tuple-element.157), channel_id=1, source_target_pairs={{0,14},{2,12},{4,10},{6,8},{8,6},{10,4},{12,2},{14,0},{16,30},{18,... | collective-permute-start | bytes 589832 | tf_op jit(solution)/shard_map/ppermute | solution.py:97
  46.5 34.0 %collective-permute-start.7 = (bf16[1,3,64,512]{3,2,1,0:T(8,128)(2,1)S(1)}, bf16[1,3,64,512]{3,2,1,0:T(8,128)(2,1)S(1)}, u32[]{:S(2)}, u32[]{:S(2)}) collective-permute-start(bf16[1,3,64,512]{3,2,1,0:T(8,128)(2,1)S(1)} %get-tuple-element.156), channel_id=1, source_target_pairs={{0,16},{2,18},{4,20},{6,22},{8,24},{10,26},{12,28},{14,30},{16,0},... | collective-permute-start | bytes 589832 | tf_op jit(solution)/shard_map/ppermute | solution.py:97
  48.3 37.7 %collective-permute-start.8 = (bf16[1,3,64,512]{3,2,1,0:T(8,128)(2,1)S(1)}, bf16[1,3,64,512]{3,2,1,0:T(8,128)(2,1)S(1)}, u32[]{:S(2)}, u32[]{:S(2)}) collective-permute-start(bf16[1,3,64,512]{3,2,1,0:T(8,128)(2,1)S(1)} %get-tuple-element.155), channel_id=1, source_target_pairs={{0,18},{2,16},{4,22},{6,20},{8,26},{10,24},{12,30},{14,28},{16,2},... | collective-permute-start | bytes 589832 | tf_op jit(solution)/shard_map/ppermute | solution.py:97
  54.5 42.0 %collective-permute-start.9 = (bf16[1,3,64,512]{3,2,1,0:T(8,128)(2,1)S(1)}, bf16[1,3,64,512]{3,2,1,0:T(8,128)(2,1)S(1)}, u32[]{:S(2)}, u32[]{:S(2)}) collective-permute-start(bf16[1,3,64,512]{3,2,1,0:T(8,128)(2,1)S(1)} %get-tuple-element.154), channel_id=1, source_target_pairs={{0,20},{2,22},{4,16},{6,18},{8,28},{10,30},{12,24},{14,26},{16,4},... | collective-permute-start | bytes 589832 | tf_op jit(solution)/shard_map/ppermute | solution.py:97
  58.9 42.3 %collective-permute-start.10 = (bf16[1,3,64,512]{3,2,1,0:T(8,128)(2,1)S(1)}, bf16[1,3,64,512]{3,2,1,0:T(8,128)(2,1)S(1)}, u32[]{:S(2)}, u32[]{:S(2)}) collective-permute-start(bf16[1,3,64,512]{3,2,1,0:T(8,128)(2,1)S(1)} %get-tuple-element.153), channel_id=1, source_target_pairs={{0,22},{2,20},{4,18},{6,16},{8,30},{10,28},{12,26},{14,24},{16,6},... | collective-permute-start | bytes 589832 | tf_op jit(solution)/shard_map/ppermute | solution.py:97
  63.3 38.6 %collective-permute-start.11 = (bf16[1,3,64,512]{3,2,1,0:T(8,128)(2,1)S(1)}, bf16[1,3,64,512]{3,2,1,0:T(8,128)(2,1)S(1)}, u32[]{:S(2)}, u32[]{:S(2)}) collective-permute-start(bf16[1,3,64,512]{3,2,1,0:T(8,128)(2,1)S(1)} %get-tuple-element.152), channel_id=1, source_target_pairs={{0,24},{2,26},{4,28},{6,30},{8,16},{10,18},{12,20},{14,22},{16,8},... | collective-permute-start | bytes 589832 | tf_op jit(solution)/shard_map/ppermute | solution.py:97
  80.5 22.1 %collective-permute-start.12 = (bf16[1,3,64,512]{3,2,1,0:T(8,128)(2,1)S(1)}, bf16[1,3,64,512]{3,2,1,0:T(8,128)(2,1)S(1)}, u32[]{:S(2)}, u32[]{:S(2)}) collective-permute-start(bf16[1,3,64,512]{3,2,1,0:T(8,128)(2,1)S(1)} %get-tuple-element.151), channel_id=1, source_target_pairs={{0,26},{2,24},{4,30},{6,28},{8,18},{10,16},{12,22},{14,20},{16,10}... | collective-permute-start | bytes 589832 | tf_op jit(solution)/shard_map/ppermute | solution.py:97
  86.0 17.3 %collective-permute-start.13 = (bf16[1,3,64,512]{3,2,1,0:T(8,128)(2,1)S(1)}, bf16[1,3,64,512]{3,2,1,0:T(8,128)(2,1)S(1)}, u32[]{:S(2)}, u32[]{:S(2)}) collective-permute-start(bf16[1,3,64,512]{3,2,1,0:T(8,128)(2,1)S(1)} %get-tuple-element.150), channel_id=1, source_target_pairs={{0,28},{2,30},{4,24},{6,26},{8,20},{10,22},{12,16},{14,18},{16,12}... | collective-permute-start | bytes 589832 | tf_op jit(solution)/shard_map/ppermute | solution.py:97
  96.4 9.4 %collective-permute-start.14 = (bf16[1,3,64,512]{3,2,1,0:T(8,128)(2,1)S(1)}, bf16[1,3,64,512]{3,2,1,0:T(8,128)(2,1)S(1)}, u32[]{:S(2)}, u32[]{:S(2)}) collective-permute-start(bf16[1,3,64,512]{3,2,1,0:T(8,128)(2,1)S(1)} %get-tuple-element.149), channel_id=1, source_target_pairs={{0,30},{2,28},{4,26},{6,24},{8,22},{10,20},{12,18},{14,16},{16,14}... | collective-permute-start | bytes 589832 | tf_op jit(solution)/shard_map/ppermute | solution.py:97
  110.8 1.2 copy-start.2
  112.1 19.4 %copy-start.5 = (u32[32]{0:T(128)S(1)}, u32[32]{0:T(128)}, u32[]{:S(2)}) copy-start(u32[32]{0:T(128)} %constant.128) | copy-start | bytes 388
  116.4 24.9 %all-to-all-start.1 = ((bf16[16,2,6144]{2,1,0:T(2,128)(2,1)}), bf16[16,2,6144]{2,1,0:T(2,128)(2,1)S(1)}, u32[]{:S(2)}, u32[]{:S(2)}) async-start(bf16[16,2,6144]{2,1,0:T(2,128)(2,1)} %reshape.335), calls=%async_computation.1 | async-start | bytes 786432 | tf_op jit(solution)/shard_map/all_to_all | solution.py:133
  147.9 3.6 copy-start.3
  147.9 3.6 copy-start.4
  151.5 3.6 copy-start
  160.9 12.3 %copy-start.1 = (bf16[8,3,64,1024]{3,2,1,0:T(8,128)(2,1)S(1)}, bf16[8,3,64,1024]{3,2,1,0:T(8,128)(2,1)}, u32[]{:S(2)}) copy-start(bf16[8,3,64,1024]{3,2,1,0:T(8,128)(2,1)} %copy-done) | copy-start | bytes 9437188 | tf_op jit(solution)/shard_map/while
  173.2 3.6 copy-start
  182.6 12.3 %copy-start.1 = (bf16[8,3,64,1024]{3,2,1,0:T(8,128)(2,1)S(1)}, bf16[8,3,64,1024]{3,2,1,0:T(8,128)(2,1)}, u32[]{:S(2)}) copy-start(bf16[8,3,64,1024]{3,2,1,0:T(8,128)(2,1)} %copy-done) | copy-start | bytes 9437188 | tf_op jit(solution)/shard_map/while
  194.9 3.6 copy-start
  204.3 12.3 %copy-start.1 = (bf16[8,3,64,1024]{3,2,1,0:T(8,128)(2,1)S(1)}, bf16[8,3,64,1024]{3,2,1,0:T(8,128)(2,1)}, u32[]{:S(2)}) copy-start(bf16[8,3,64,1024]{3,2,1,0:T(8,128)(2,1)} %copy-done) | copy-start | bytes 9437188 | tf_op jit(solution)/shard_map/while
  216.6 3.6 copy-start
  226.0 12.3 %copy-start.1 = (bf16[8,3,64,1024]{3,2,1,0:T(8,128)(2,1)S(1)}, bf16[8,3,64,1024]{3,2,1,0:T(8,128)(2,1)}, u32[]{:S(2)}) copy-start(bf16[8,3,64,1024]{3,2,1,0:T(8,128)(2,1)} %copy-done) | copy-start | bytes 9437188 | tf_op jit(solution)/shard_map/while
  238.3 3.6 copy-start
  247.7 12.3 %copy-start.1 = (bf16[8,3,64,1024]{3,2,1,0:T(8,128)(2,1)S(1)}, bf16[8,3,64,1024]{3,2,1,0:T(8,128)(2,1)}, u32[]{:S(2)}) copy-start(bf16[8,3,64,1024]{3,2,1,0:T(8,128)(2,1)} %copy-done) | copy-start | bytes 9437188 | tf_op jit(solution)/shard_map/while
  260.0 3.6 copy-start
  269.4 12.3 %copy-start.1 = (bf16[8,3,64,1024]{3,2,1,0:T(8,128)(2,1)S(1)}, bf16[8,3,64,1024]{3,2,1,0:T(8,128)(2,1)}, u32[]{:S(2)}) copy-start(bf16[8,3,64,1024]{3,2,1,0:T(8,128)(2,1)} %copy-done) | copy-start | bytes 9437188 | tf_op jit(solution)/shard_map/while
  281.7 3.6 copy-start
  291.1 12.3 %copy-start.1 = (bf16[8,3,64,1024]{3,2,1,0:T(8,128)(2,1)S(1)}, bf16[8,3,64,1024]{3,2,1,0:T(8,128)(2,1)}, u32[]{:S(2)}) copy-start(bf16[8,3,64,1024]{3,2,1,0:T(8,128)(2,1)} %copy-done) | copy-start | bytes 9437188 | tf_op jit(solution)/shard_map/while
  303.4 3.6 copy-start
  312.8 12.3 %copy-start.1 = (bf16[8,3,64,1024]{3,2,1,0:T(8,128)(2,1)S(1)}, bf16[8,3,64,1024]{3,2,1,0:T(8,128)(2,1)}, u32[]{:S(2)}) copy-start(bf16[8,3,64,1024]{3,2,1,0:T(8,128)(2,1)} %copy-done) | copy-start | bytes 9437188 | tf_op jit(solution)/shard_map/while
  325.1 42.4 %copy-start.6 = (f32[8]{0:T(128)}, f32[8]{0:T(128)S(1)}, u32[]{:S(2)}) copy-start(f32[8]{0:T(128)S(1)} %get-tuple-element.57) | copy-start | bytes 100
Sparse Core Ops, SparseCore 0:
  111.0 26.1 all-gather.2
